TPU v7x, 32 devices: a whole 2x2x4 slice. The times are simulated.
32 devices in a mesh: layer: 2 (over y), latent: 8 (over z, x), tok: 2 (over core).
Axes of the slice: x: 2, y: 2, z: 4, core: 2. Of those that a mesh axis runs over, the one named last changes fastest.
Arguments:
- resid: bfloat16 [2, 384, 2304], P('layer', 'tok', 'latent'), may hold values from -6 to 6
- w_enc: bfloat16 [2, 2304, 2048], P('layer', None, 'latent'), may hold values from -0.09375 to 0.09375
- b_enc: float32 [2048], P('latent'), may hold values from -3 to 3
- w_dec: bfloat16 [2, 2048, 2304], P('layer', 'latent'), may hold values from -0.125 to 0.125
- b_dec: bfloat16 [2, 2304], P('layer', 'latent'), may hold values from -3 to 3
Outputs:
- grad_w_enc: bfloat16 [2, 2304, 2048], P('layer', 'tok', 'latent')
- grad_w_dec: bfloat16 [2, 2048, 2304], P('layer', 'latent')
All inputs are finite; a program needn't handle non-finite values.
Results may differ from a plain program's by a relative error of at most 0.023.
Values may be sent and summed in bfloat16 or wider, within the bound.
A program may use at most 64 MiB of HBM per device.

v0:
```python
import jax
import jax.numpy as jnp
from jax import lax
from jax.sharding import PartitionSpec as P

BETA = 4.0


def shards(resid, w_enc, b_enc, w_dec, b_dec):
    decoder = w_dec[0]
    x_full, bias_full = (
        lax.all_gather(resid, "latent", axis=2, tiled=True),
        lax.all_gather(b_dec.reshape(1, 1, -1), "latent", axis=2, tiled=True),
    )
    x_full = x_full[0]
    bias_full = bias_full.reshape(-1).astype(jnp.float32)
    tok_rows = x_full.shape[0]
    tokens = tok_rows * lax.axis_size("tok")
    partial_value = jnp.dot(x_full, w_enc[0], preferred_element_type=jnp.float32)
    pre = lax.psum(partial_value.astype(jnp.bfloat16), "layer").astype(jnp.float32) + b_enc
    act = (jax.nn.softplus(BETA * pre) / BETA).astype(jnp.bfloat16)
    slope = jax.nn.sigmoid(BETA * pre)
    recon = lax.psum(
        jnp.dot(act, decoder, preferred_element_type=jnp.float32).astype(jnp.bfloat16), "latent"
    ).astype(jnp.float32)
    grad_all = (2.0 / tokens * (recon + bias_full - x_full.astype(jnp.float32))).astype(
        jnp.bfloat16
    )
    dec_sum = lax.dot_general(
        act, grad_all, (((0,), (0,)), ((), ())), preferred_element_type=jnp.float32
    )
    rows_grad = lax.dot_general(
        grad_all, decoder, (((1,), (1,)), ((), ())), preferred_element_type=jnp.float32
    )
    act_grad = rows_grad
    dec_sum, act_grad = (dec_sum, act_grad)
    grad_act = lax.psum(act_grad.astype(jnp.bfloat16), "layer").astype(jnp.float32)
    grad_pre = (grad_act * slope).astype(jnp.bfloat16)
    grad_w_dec = lax.psum(dec_sum.astype(jnp.bfloat16), "tok")
    grad_w_enc = lax.psum_scatter(
        lax.dot_general(
            x_full, grad_pre, (((0,), (0,)), ((), ())), preferred_element_type=jnp.float32
        ).astype(jnp.bfloat16),
        "tok",
        scatter_dimension=0,
        tiled=True,
    )
    return (grad_w_enc[None], grad_w_dec[None])


def solution(mesh):
    placed = (
        P("layer", "tok", "latent"),
        P("layer", None, "latent"),
        P("latent"),
        P("layer", "latent", None),
        P("layer", "latent"),
    )
    return jax.shard_map(
        shards,
        mesh=mesh,
        in_specs=placed,
        out_specs=(P("layer", "tok", "latent"), P("layer", "latent", None)),
        check_vma=False,
    )
```

profile of v0, /device:TPU:1, one launch (start us, length us, event | category | flops | bytes accessed | tf_op | source)
XLA Modules:
  0.0 234.8 jit_solution(12181217095717214668)
XLA Ops:
  7.2 1.9 copy.8
  9.1 50.1 %all_gather.6 = bf16[1,192,2304]{1,0,2:T(2,128)(2,1)S(1)} all-gather(bf16[1,192,288]{1,0,2:T(2,128)(2,1)} %copy.8), channel_id=1, replica_groups=mesh['layer'=2,'latent'=8,'tok'=2] {'latent'}, dimensions={2}, use_global_device_ids=true | all-gather | bytes 995328 | tf_op jit(solution)/shard_map/all_gather | solution.py:12
  59.2 4.9 %copy.9 = bf16[1,192,2304]{2,1,0:T(8,128)(2,1)} copy(bf16[1,192,2304]{1,0,2:T(2,128)(2,1)S(1)} %all_gather.6) | data formatting | bytes 1769472 | tf_op jit(solution)/shard_map/all_gather | solution.py:12
  64.1 2.6 %fusion.7 = bf16[192,256]{1,0:T(8,128)(2,1)} fusion(bf16[1,2304,256]{2,1,0:T(8,128)(2,1)} %param.6, bf16[1,192,2304]{2,1,0:T(8,128)(2,1)} %copy.9), kind=kOutput, calls=%fused_computation.11 | convolution fusion | flops 226541568 | bytes 2162688 | tf_op jit(solution)/shard_map/dot_general | solution.py:19
  66.7 0.0 all-reduce.8.cloned.1.call-start
  66.8 20.4 %all-reduce.6.cloned.1.call-done = bf16[192,256]{1,0:T(8,128)(2,1)} async-done(((bf16[192,256]{1,0:T(8,128)(2,1)}), bf16[192,256]{1,0:T(8,128)(2,1)}) %all-reduce.6.cloned.1.call-update) | async-done | bytes 98320 | tf_op jit(solution)/shard_map/psum | solution.py:20
  87.2 2.3 convolution_convert_fusion.2
  89.5 0.0 all-reduce.10.cloned.1.call-start
  89.6 0.6 dynamic-slice
  90.9 0.3 dynamic-update-slice
  91.1 18.3 %all-reduce = bf16[2304]{0:T(1024)(128)(2,1)S(1)} all-reduce(bf16[2304]{0:T(1024)(128)(2,1)S(1)} %dynamic-update-slice), channel_id=2, replica_groups=mesh['layer'=2,'latent'=8,'tok'=2] {'latent'}, use_global_device_ids=true, to_apply=%add | all-reduce | flops 2304 | bytes 9216
  109.4 57.1 %all-reduce.8.cloned.1.call-done = bf16[192,2304]{1,0:T(8,128)(2,1)} async-done(((bf16[192,2304]{1,0:T(8,128)(2,1)}), bf16[192,2304]{1,0:T(8,128)(2,1)}) %all-reduce.8.cloned.1.call-update) | async-done | bytes 884752 | tf_op jit(solution)/shard_map/psum | solution.py:23
  166.6 2.4 %fusion.10 = bf16[192,256]{1,0:T(8,128)(2,1)} fusion(bf16[1,256,2304]{2,1,0:T(8,128)(2,1)S(1)} %copy-done, bf16[192,2304]{1,0:T(8,128)(2,1)} %all-reduce.8.cloned.1.call-done, bf16[1,192,2304]{2,1,0:T(8,128)(2,1)S(1)} %copy-done.1, f32[2304]{0:T(1024)S(1)} %convert_element_type.66), kind=kOutput, calls=%fused_computation.12 | convolution fusion | flops 229195776 | bytes 3056640 | tf_op jit(solution)/shard_map/dot_general | solution.py:32
  169.0 0.0 reduce-scatter.4.cloned.1.call-start
  169.0 21.3 %all-reduce.10.cloned.1.call-done = bf16[192,256]{1,0:T(8,128)(2,1)} async-done(((bf16[192,256]{1,0:T(8,128)(2,1)}), bf16[192,256]{1,0:T(8,128)(2,1)}) %all-reduce.10.cloned.1.call-update) | async-done | bytes 98320 | tf_op jit(solution)/shard_map/psum | solution.py:37
  190.3 1.4 fusion
  191.7 1.4 copy.11
  193.2 0.0 all-reduce.12.cloned.1.call-start
  193.2 2.9 %fusion.1 = bf16[1,256,2304]{2,1,0:T(8,128)(2,1)} fusion(bf16[192,2304]{1,0:T(8,128)(2,1)} %all-reduce.8.cloned.1.call-done, bf16[1,192,2304]{2,1,0:T(8,128)(2,1)S(1)} %copy-done.1, f32[2304]{0:T(1024)S(1)} %convert_element_type.66, bf16[192,256]{1,0:T(8,128)(2,1)S(1)} %copy-done.2, f32[256]{0:T(256)S(1)} %copy-done.4), kind=kOutput, calls=%fused_computation.4 | convolution fusion | flops 230277120 | bytes 3057664 | tf_op jit(solution)/shard_map/dot_general | solution.py:29
  196.1 6.7 %reduce-scatter.4.cloned.1.call-done = bf16[1152,256]{1,0:T(8,128)(2,1)} async-done(((bf16[2304,256]{1,0:T(8,128)(2,1)}), bf16[1152,256]{1,0:T(8,128)(2,1)}) %reduce-scatter.4.cloned.1.call-update) | async-done | bytes 589840
  202.8 1.4 copy.12
  204.2 1.1 copy.10
  205.3 20.6 %all-reduce.12.cloned.1.call-done = bf16[1,256,2304]{2,1,0:T(8,128)(2,1)} async-done(((bf16[1,256,2304]{2,1,0:T(8,128)(2,1)}), bf16[1,256,2304]{2,1,0:T(8,128)(2,1)}) %all-reduce.12.cloned.1.call-update) | async-done | bytes 1179664 | tf_op jit(solution)/shard_map/psum | solution.py:39
  225.9 2.4 %copy.18 = bf16[1,256,2304]{2,1,0:T(8,128)(2,1)} copy(bf16[1,256,2304]{2,1,0:T(8,128)(2,1)} %all-reduce.12.cloned.1.call-done) | data formatting | bytes 2359296
  (21 shorter events, 0.2 us)
Async XLA Ops:
  7.2 80.0 %copy-start = (bf16[1,256,2304]{2,1,0:T(8,128)(2,1)S(1)}, bf16[1,256,2304]{2,1,0:T(8,128)(2,1)}, u32[]{:S(2)}) copy-start(bf16[1,256,2304]{2,1,0:T(8,128)(2,1)} %param.8) | copy-start | bytes 3538948
  7.2 80.0 %all-reduce.6.cloned.1.call-start = ((), (), s32[]{:S(2)}) async-start(), calls=%async_computation.1 | async-start | bytes 196608 | tf_op jit(solution)/shard_map/psum | solution.py:20
  64.1 23.1 %copy-start.4 = (f32[256]{0:T(256)S(1)}, f32[256]{0:T(256)}, u32[]{:S(2)}) copy-start(f32[256]{0:T(256)} %param.7) | copy-start | bytes 3076
  66.7 22.9 %copy-start.5 = (u32[32]{0:T(128)S(1)}, u32[32]{0:T(128)}, u32[]{:S(2)}) copy-start(u32[32]{0:T(128)} %constant.17) | copy-start | bytes 388
  66.7 24.2 %copy-start.3 = (bf16[1,288]{1,0:T(2,128)(2,1)S(1)}, bf16[1,288]{1,0:T(2,128)(2,1)}, u32[]{:S(2)}) copy-start(bf16[1,288]{1,0:T(2,128)(2,1)} %param.9) | copy-start | bytes 1732
  66.7 99.9 %copy-start.1 = (bf16[1,192,2304]{2,1,0:T(8,128)(2,1)S(1)}, bf16[1,192,2304]{2,1,0:T(8,128)(2,1)}, u32[]{:S(2)}) copy-start(bf16[1,192,2304]{2,1,0:T(8,128)(2,1)} %copy.9) | copy-start | bytes 2654212
  66.7 99.9 %all-reduce.8.cloned.1.call-start = ((), (), s32[]{:S(2)}) async-start(), calls=%async_computation.2 | async-start | bytes 1769472 | tf_op jit(solution)/shard_map/psum | solution.py:23
  89.5 100.7 %all-reduce.10.cloned.1.call-start = ((), (), s32[]{:S(2)}) async-start(), calls=%async_computation.3 | async-start | bytes 196608 | tf_op jit(solution)/shard_map/psum | solution.py:37
  109.4 80.9 %copy-start.2 = (bf16[192,256]{1,0:T(8,128)(2,1)S(1)}, bf16[192,256]{1,0:T(8,128)(2,1)}, u32[]{:S(2)}) copy-start(bf16[192,256]{1,0:T(8,128)(2,1)} %all-reduce.6.cloned.1.call-done) | copy-start | bytes 294916
  169.0 33.9 %reduce-scatter.4.cloned.1.call-start = ((), (), s32[]{:S(2)}) async-start(), calls=%async_computation.5 | async-start | bytes 1769472
  193.2 32.7 %all-reduce.12.cloned.1.call-start = ((), (), s32[]{:S(2)}) async-start(), calls=%async_computation.4 | async-start | bytes 2359296 | tf_op jit(solution)/shard_map/psum | solution.py:39
Sparse Core Ops, SparseCore 0:
  66.8 20.3 all-reduce.5
  90.7 75.8 all-reduce.7
  169.4 20.8 all-reduce.9
  193.3 9.4 reduce-scatter.3
  205.0 20.8 all-reduce.11
where the time goes:
time: 235 us
  waiting for transfers between devices  126 us (54%)
  blocking collectives  68.3 us (29%)
  between operations  14.5 us (6%)
  local copies, waits for them, and re-layouts  13.9 us (6%)
  matrix products  11.6 us (5%)
    psum x1, waiting for transfers between devices, shards(): lax.psum(jnp.dot(act, decoder, preferred_element_type=jnp.float32).astype...  57.1 us
    all_gather x1, blocking collectives, shards(): lax.all_gather(resid, 'latent', axis=2, tiled=True)  50.1 us
    psum x1, waiting for transfers between devices, shards(): lax.psum(act_grad.astype(jnp.bfloat16), 'layer').astype(jnp.float32)  21.3 us
    psum x1, waiting for transfers between devices, shards(): grad_w_dec = lax.psum(dec_sum.astype(jnp.bfloat16), 'tok')  20.6 us
    psum x1, waiting for transfers between devices, shards(): lax.psum(partial_value.astype(jnp.bfloat16), 'layer').astype(jnp.float32)  20.4 us
    unnamed x1, blocking collectives  18.3 us
    unnamed x20, local copies, waits for them, and re-layouts  8.98 us
    unnamed x6, waiting for transfers between devices  6.77 us
  transfers between devices with their start and end apart: 5, of which 5 were waited for; matrix products, arithmetic and copies ran while one was open for 3% of the time, Pallas kernels for 0%

commit v1 on v0

v1 whole, which is shorter than its diff:
```python
import functools

import jax
import jax.numpy as jnp
from jax import lax
from jax.experimental import pallas as pl
from jax.experimental.pallas import tpu as pltpu
from jax.sharding import PartitionSpec as P

BETA = 4.0
LANES = 128
MESH = pl.DeviceIdType.MESH
F32 = jnp.float32
BF16 = jnp.bfloat16


def plain_shards(resid, w_enc, b_enc, w_dec, b_dec):
    decoder = w_dec[0]
    x_full = lax.all_gather(resid, "latent", axis=2, tiled=True)[0]
    bias_full = lax.all_gather(b_dec.reshape(1, 1, -1), "latent", axis=2, tiled=True)
    bias_full = bias_full.reshape(-1).astype(F32)
    tokens = x_full.shape[0] * lax.axis_size("tok")
    partial_value = jnp.dot(x_full, w_enc[0], preferred_element_type=F32)
    pre = lax.psum(partial_value.astype(BF16), "layer").astype(F32) + b_enc
    act = (jax.nn.softplus(BETA * pre) / BETA).astype(BF16)
    slope = jax.nn.sigmoid(BETA * pre)
    recon = lax.psum(
        jnp.dot(act, decoder, preferred_element_type=F32).astype(BF16), "latent"
    ).astype(F32)
    grad_all = (2.0 / tokens * (recon + bias_full - x_full.astype(F32))).astype(BF16)
    dec_sum = lax.dot_general(
        act, grad_all, (((0,), (0,)), ((), ())), preferred_element_type=F32
    )
    act_grad = lax.dot_general(
        grad_all, decoder, (((1,), (1,)), ((), ())), preferred_element_type=F32
    )
    grad_act = lax.psum(act_grad.astype(BF16), "layer").astype(F32)
    grad_pre = (grad_act * slope).astype(BF16)
    grad_w_dec = lax.psum(dec_sum.astype(BF16), "tok")
    grad_w_enc = lax.psum_scatter(
        lax.dot_general(
            x_full, grad_pre, (((0,), (0,)), ((), ())), preferred_element_type=F32
        ).astype(BF16),
        "tok",
        scatter_dimension=0,
        tiled=True,
    )
    return (grad_w_enc[None], grad_w_dec[None])


def kernel(
    n_lat, tokens,
    x_ref, we_hbm, be_ref, wd_hbm, bd_ref,
    oe_ref, od_ref,
    we, wdv, wd, xb, xo, xt, gb, go, pre, slope, act, act_t, act_o, ys, yr, hs, hr, gp, gp_o,
    xs, xr, zs, zr,
    load_sem, x_ss, x_rs, xo_rs, g_ss, g_rs, go_rs, one_ss, one_rs, xs_ss, xr_rs, zs_ss, zr_rs,
):
    rows, feats = x_ref.shape
    hid = we.shape[1]
    main = feats // LANES * LANES
    tiles = main // LANES
    rest = feats - main
    groups = LANES // rest
    sub = rows // groups
    nz = n_lat // 2
    half = n_lat // 2

    lay = lax.axis_index("layer")
    lat = lax.axis_index("latent")
    tok = lax.axis_index("tok")
    z, xx = lat // 2, lat % 2
    across = 2 * z + 1 - xx
    lay_o, tok_o = 1 - lay, 1 - tok

    we_load = pltpu.make_async_copy(we_hbm, we, load_sem.at[0])
    wd_load = pltpu.make_async_copy(wd_hbm, wdv, load_sem.at[1])
    we_load.start()
    wd_load.start()

    barrier = pltpu.get_barrier_semaphore()
    for d in range(1, nz):
        pl.semaphore_signal(
            barrier, inc=1, device_id={"latent": 2 * ((z + d) % nz) + xx}, device_id_type=MESH
        )
    pl.semaphore_signal(barrier, inc=1, device_id={"latent": across}, device_id_type=MESH)
    pl.semaphore_signal(barrier, inc=1, device_id={"layer": lay_o}, device_id_type=MESH)
    pl.semaphore_signal(barrier, inc=1, device_id={"tok": tok_o}, device_id_type=MESH)

    def remote(src, dst, ss, rs, where):
        return pltpu.make_async_remote_copy(
            src_ref=src, dst_ref=dst, send_sem=ss, recv_sem=rs,
            device_id=where, device_id_type=MESH,
        )

    lane = lax.broadcasted_iota(jnp.int32, (sub, LANES), 1) // rest

    def pack(full):
        out = jnp.zeros((sub, LANES), F32)
        for g in range(groups):
            out = jnp.where(lane == g, full[g * sub:(g + 1) * sub, main:], out)
        return jnp.concatenate(
            [full[:, i * LANES:(i + 1) * LANES] for i in range(tiles)] + [out], axis=0
        )

    def spread(block):
        packed = block[tiles * rows:]
        zero = jnp.zeros_like(packed)
        parts = jnp.concatenate(
            [jnp.where(lane == g, packed, zero) for g in range(groups)], axis=0
        )
        return jnp.concatenate(
            [block[i * rows:(i + 1) * rows] for i in range(tiles)] + [parts], axis=1
        )

    def gather(buf, ss, rs, use, to_tok):
        def up(j):
            return remote(buf.at[j], buf.at[j], ss.at[0, j], rs.at[j], {"latent": lat + 2})

        def down(j):
            return remote(buf.at[j], buf.at[j], ss.at[1, j], rs.at[j], {"latent": lat - 2})

        def side(j):
            return remote(buf.at[j], buf.at[j], ss.at[2, j], rs.at[j], {"latent": across})

        @pl.when(z < nz - 1)
        def _():
            up(lat).start()

        @pl.when(z > 0)
        def _():
            down(lat).start()

        side(lat).start()
        to_tok(lat)
        use(lat)

        def far(s):
            @pl.when(z - s >= 0)
            def _():
                j = across - 2 * s
                side(j).wait_recv()
                to_tok(j)
                use(j)

            @pl.when(z + s < nz)
            def _():
                j = across + 2 * s
                side(j).wait_recv()
                to_tok(j)
                use(j)

        for s in range(1, nz):
            @pl.when(z - s >= 0)
            def _():
                j = lat - 2 * s
                side(j).wait_recv()

                @pl.when(z < nz - 1)
                def _():
                    up(j).start()

                side(j).start()
                to_tok(j)
                use(j)

            @pl.when(z + s < nz)
            def _():
                j = lat + 2 * s
                side(j).wait_recv()

                @pl.when(z > 0)
                def _():
                    down(j).start()

                side(j).start()
                to_tok(j)
                use(j)

            if s == 1:
                side(across).wait_recv()
                to_tok(across)
                use(across)
            else:
                far(s - 1)
        far(nz - 1)

        def finish():
            side(lat).wait_send()

            @pl.when(z < nz - 1)
            def _():
                up(lat).wait_send()

            @pl.when(z > 0)
            def _():
                down(lat).wait_send()

            for s in range(1, nz):
                @pl.when(z - s >= 0)
                def _():
                    j = lat - 2 * s
                    side(j).wait_send()

                    @pl.when(z < nz - 1)
                    def _():
                        up(j).wait_send()

                @pl.when(z + s < nz)
                def _():
                    j = lat + 2 * s
                    side(j).wait_send()

                    @pl.when(z > 0)
                    def _():
                        down(j).wait_send()

        return finish

    tail = x_ref[:, main:]
    wide = jnp.concatenate([x_ref[:, :main]] + [tail] * groups, axis=1)
    xb[lat] = pack(wide.astype(F32)).astype(BF16)
    pre[...] = jnp.zeros_like(pre)

    pl.semaphore_wait(barrier, nz + 2)

    def x_tok(i):
        return remote(
            xb.at[half * tok_o + i], xo.at[i], x_ss.at[3, i], xo_rs.at[i], {"tok": tok_o}
        )

    def x_to_tok(j):
        @pl.when(j // half == tok_o)
        def _():
            x_tok(j - half * tok_o).start()

    def encode(j):
        lo = pl.multiple_of(j * feats, rest)
        w_main = we[pl.ds(lo, main), :]
        w_rest = we[pl.ds(pl.multiple_of(lo + main, rest), rest), :]
        w = jnp.concatenate([w_main] + [w_rest] * groups, axis=0)
        pre[...] += jnp.dot(spread(xb[j]), w, preferred_element_type=F32)

    first = []

    def encode_first(j):
        if not first:
            first.append(1)
            we_load.wait()
            encode(j)
            wd_load.wait()
            for k in range(n_lat):
                lo = k * feats
                w_rest = wdv[:, lo + main:lo + feats]
                wd[k] = jnp.concatenate([wdv[:, lo:lo + main]] + [w_rest] * groups, axis=1)
        else:
            encode(j)

    x_done = gather(xb, x_ss, x_rs, encode_first, x_to_tok)

    ys[...] = pre[...].astype(BF16)
    y_copy = remote(ys, yr, one_ss.at[0], one_rs.at[0], {"layer": lay_o})
    y_copy.start()
    y_copy.wait_recv()
    v = BETA * (pre[...] + yr[...].astype(F32) + be_ref[...])
    e = jnp.exp(-jnp.abs(v))
    act[...] = ((jnp.maximum(v, 0.0) + jnp.log1p(e)) / BETA).astype(BF16)
    slope[...] = jnp.where(v >= 0, 1.0, e) / (1.0 + e)

    def other(k):
        hi = z // (nz // 2)
        m = z + hi * (nz - 1 - 2 * z)
        if k == nz - 1:
            return z
        vv = nz - 1 - k - (m + k) // (nz - 1)
        return vv + hi * (nz - 1 - 2 * vv)

    def x_send(zt):
        return remote(xs.at[zt], xr.at[zt], xs_ss.at[zt], xr_rs.at[zt], {"latent": across})

    def z_send(zt):
        return remote(zs.at[zt], zr.at[z], zs_ss.at[zt], zr_rs.at[z], {"latent": 2 * zt + xx})

    def z_recv(zt):
        return remote(zs.at[zt], zr.at[zt], zs_ss.at[zt], zr_rs.at[zt], {"latent": 2 * zt + xx})

    def decode(j):
        return pack(jnp.dot(act[...], wd[j], preferred_element_type=F32))

    for k in range(nz):
        zt = other(k)
        xs[zt] = decode(2 * zt + 1 - xx).astype(BF16)
        x_send(zt).start()
    a_copy = remote(act, act_o, one_ss.at[1], one_rs.at[1], {"tok": tok_o})
    a_copy.start()
    for k in range(nz - 1):
        zt = other(k)
        mine = decode(2 * zt + xx)
        x_send(zt).wait_recv()
        zs[zt] = (mine + xr[zt].astype(F32)).astype(BF16)
        z_send(zt).start()
    total = decode(lat)
    bias = bd_ref[...].astype(F32)
    bias = jnp.concatenate([bias[:, :main]] + [bias[:, main:]] * groups, axis=1)
    total += jnp.concatenate(
        [jnp.broadcast_to(bias[:, i * LANES:(i + 1) * LANES], (rows, LANES)) for i in range(tiles)]
        + [jnp.broadcast_to(bias[:, main:], (sub, LANES))],
        axis=0,
    ) - xb[lat].astype(F32)
    for i in range(half):
        x_tok(i).wait_recv()
        both = jnp.concatenate([spread(xb[half * tok + i]), spread(xo[i])], axis=0)
        xt[i] = both.T
    a_copy.wait_recv()
    act_t[...] = jnp.concatenate([act[...], act_o[...]], axis=0).T
    x_send(z).wait_recv()
    total += xr[z].astype(F32)
    for k in reversed(range(nz - 1)):
        zt = other(k)
        z_recv(zt).wait_recv()
        total += zr[zt].astype(F32)
    gb[lat] = (2.0 / tokens * total).astype(BF16)
    pre[...] = jnp.zeros_like(pre)

    def g_tok(j):
        return remote(gb.at[j], go.at[j], g_ss.at[3, j], go_rs.at[j], {"tok": tok_o})

    def g_to_tok(j):
        g_tok(j).start()

    def back(j):
        pre[...] += lax.dot_general(
            spread(gb[j]), wd[j], (((1,), (1,)), ((), ())), preferred_element_type=F32
        )

    g_done = gather(gb, g_ss, g_rs, back, g_to_tok)

    hs[...] = pre[...].astype(BF16)
    h_copy = remote(hs, hr, one_ss.at[2], one_rs.at[2], {"layer": lay_o})
    h_copy.start()

    row = []
    for j in range(n_lat):
        g_tok(j).wait_recv()
        both = jnp.concatenate([spread(gb[j]), spread(go[j])], axis=0)
        dw = jnp.dot(act_t[...], both, preferred_element_type=F32)
        r = dw[:, main:main + rest]
        for g in range(1, groups):
            r = r + dw[:, main + g * rest:main + (g + 1) * rest]
        row += [dw[:, :main], r]
        if (j + 1) * feats % LANES == 0:
            width = sum(p.shape[1] for p in row)
            od_ref[:, (j + 1) * feats - width:(j + 1) * feats] = jnp.concatenate(
                row, axis=1
            ).astype(BF16)
            row = []

    h_copy.wait_recv()
    gp[...] = ((pre[...] + hr[...].astype(F32)) * slope[...]).astype(BF16)
    p_copy = remote(gp, gp_o, one_ss.at[3], one_rs.at[3], {"tok": tok_o})
    p_copy.start()
    p_copy.wait_recv()
    gp_both = jnp.concatenate([gp[...], gp_o[...]], axis=0)
    for i in range(half):
        dw = jnp.dot(xt[i], gp_both, preferred_element_type=F32)
        r = dw[main:main + rest]
        for g in range(1, groups):
            r = r + dw[main + g * rest:main + (g + 1) * rest]
        oe_ref[i * feats:(i + 1) * feats] = jnp.concatenate([dw[:main], r], axis=0).astype(BF16)

    x_done()
    g_done()
    for i in range(half):
        x_tok(i).wait_send()
    for j in range(n_lat):
        g_tok(j).wait_send()
    y_copy.wait_send()
    a_copy.wait_send()
    h_copy.wait_send()
    p_copy.wait_send()
    for k in range(nz):
        x_send(other(k)).wait_send()
    for k in range(nz - 1):
        z_send(other(k)).wait_send()


def fused_shards(n_lat, resid, w_enc, b_enc, w_dec, b_dec):
    x, we, wd = resid[0], w_enc[0], w_dec[0]
    rows, feats = x.shape
    total, hid = we.shape
    main = feats // LANES * LANES
    wide = main + LANES
    block = rows * feats // LANES
    half, nz = n_lat // 2, n_lat // 2
    dma = pltpu.SemaphoreType.DMA
    vm = pltpu.VMEM
    blocks = vm((n_lat, block, LANES), BF16)
    blocks_z = vm((nz, block, LANES), BF16)
    square = vm((rows, hid), BF16)
    in_vmem = pl.BlockSpec(memory_space=pltpu.VMEM)
    anywhere = pl.BlockSpec(memory_space=pl.ANY)
    ge, gd = pl.pallas_call(
        functools.partial(kernel, n_lat, rows * 2),
        out_shape=(
            jax.ShapeDtypeStruct((half * feats, hid), BF16),
            jax.ShapeDtypeStruct((hid, total), BF16),
        ),
        in_specs=[in_vmem, anywhere, in_vmem, anywhere, in_vmem],
        out_specs=(in_vmem, in_vmem),
        scratch_shapes=[
            vm((total, hid), BF16),
            vm((hid, total), BF16),
            vm((n_lat, hid, wide), BF16),
            blocks,
            vm((half, block, LANES), BF16),
            vm((half, wide, 2 * rows), BF16),
            blocks, blocks,
            vm((rows, hid), F32), vm((rows, hid), F32),
            square, vm((hid, 2 * rows), BF16), square,
            square, square, square, square, square, square,
            blocks_z, blocks_z, blocks_z, blocks_z,
            dma((2,)),
            dma((4, n_lat)), dma((n_lat,)), dma((half,)),
            dma((4, n_lat)), dma((n_lat,)), dma((n_lat,)),
            dma((4,)), dma((4,)),
            dma((nz,)), dma((nz,)), dma((nz,)), dma((nz,)),
        ],
        compiler_params=pltpu.CompilerParams(
            collective_id=0, has_side_effects=True, vmem_limit_bytes=48 * 2**20
        ),
    )(x, we, b_enc.reshape(1, -1), wd, b_dec)
    return ge[None], gd[None]


def packs(mesh, rows, feats):
    rest = feats % LANES
    if mesh.shape["layer"] != 2 or mesh.shape["tok"] != 2 or mesh.shape["latent"] % 4:
        return False
    if rest == 0 or rest % 32 or LANES % rest:
        return False
    return rows % (16 * (LANES // rest)) == 0 and feats > LANES


def solution(mesh):
    def shards(resid, w_enc, b_enc, w_dec, b_dec):
        _, rows, feats = resid.shape
        if packs(mesh, rows, feats) and resid.shape[0] == 1:
            return fused_shards(mesh.shape["latent"], resid, w_enc, b_enc, w_dec, b_dec)
        return plain_shards(resid, w_enc, b_enc, w_dec, b_dec)

    placed = (
        P("layer", "tok", "latent"),
        P("layer", None, "latent"),
        P("latent"),
        P("layer", "latent", None),
        P("layer", "latent"),
    )
    return jax.shard_map(
        shards,
        mesh=mesh,
        in_specs=placed,
        out_specs=(P("layer", "tok", "latent"), P("layer", "latent", None)),
        check_vma=False,
    )
```

time: 235 us -> 66.4 us (0.28)
  waiting for transfers between devices: 126 us -> 0 us
  blocking collectives: 68.3 us -> 0 us
  Pallas kernels: 0 us -> 58.9 us
  between operations: 14.5 us -> 0.65 us
  matrix products: 11.6 us -> 0 us
  local copies, waits for them, and re-layouts: 13.9 us -> 6.63 us
    psum x4 -> x0, waiting for transfers between devices: 119 us -> none  [the longest x1 57.1 us: shards(): lax.psum(jnp.dot(act, decoder, preferred_element_type=jnp.float32).astype...]
    pallas_call x0 -> x1, Pallas kernels: none -> 58.9 us  [fused_shards(): pl.pallas_call(functools.partial(kernel, n_lat, rows * 2), out_shape=(jax...]
    all_gather x1 -> x0, blocking collectives: 50.1 us -> none  [shards(): lax.all_gather(resid, 'latent', axis=2, tiled=True)]
    unnamed x1 -> x0, blocking collectives: 18.3 us -> none
    dot_general x5 -> x0, matrix products: 11.6 us -> none  [the longest x1 2.88 us: shards(): lax.dot_general(act, grad_all, (((0,), (0,)), ((), ())), preferred_elemen...]
    unnamed x6 -> x0, waiting for transfers between devices: 6.77 us -> none
    all_gather x1 -> x0, local copies, waits for them, and re-layouts: 4.88 us -> none  [shards(): lax.all_gather(resid, 'latent', axis=2, tiled=True)]
    unnamed x20 -> x12, local copies, waits for them, and re-layouts: 8.98 us -> 6.63 us
  transfers between devices with their start and end apart: 5 -> 0, of which waited for: 5 -> 0; matrix products, arithmetic and copies ran while one was open for 3% -> 0% of each run, Pallas kernels for 0% -> 0%
where the time goes in v1:
time: 66.4 us; the launch traced here: 66.2 us
  Pallas kernels  58.9 us (89%)
  local copies, waits for them, and re-layouts  6.63 us (10%)
    pallas_call x1, Pallas kernels, fused_shards(): pl.pallas_call(functools.partial(kernel, n_lat, rows * 2), out_shape=(jax...  58.9 us
    unnamed x12, local copies, waits for them, and re-layouts  6.63 us

profile of v1, /device:TPU:1, one launch (start us, length us, event | category | flops | bytes accessed | tf_op | source)
XLA Modules:
  0.0 66.2 jit_solution(7624261823138149820)
XLA Ops:
  0.6 0.0 copy-start
  0.6 1.3 %copy-done = bf16[1,2304,256]{2,1,0:T(8,128)(2,1)S(1)} copy-done((bf16[1,2304,256]{2,1,0:T(8,128)(2,1)S(1)}, bf16[1,2304,256]{2,1,0:T(8,128)(2,1)}, u32[]{:S(2)}) %copy-start) | copy-done | bytes 1179672
  1.9 0.0 copy-start.1
  1.9 1.3 %copy-done.1 = bf16[1,256,2304]{2,1,0:T(8,128)(2,1)S(1)} copy-done((bf16[1,256,2304]{2,1,0:T(8,128)(2,1)S(1)}, bf16[1,256,2304]{2,1,0:T(8,128)(2,1)}, u32[]{:S(2)}) %copy-start.1) | copy-done | bytes 1179672
  3.2 0.0 copy-start.2
  3.2 0.9 %copy-done.2 = bf16[1,192,288]{2,1,0:T(8,128)(2,1)S(1)} copy-done((bf16[1,192,288]{2,1,0:T(8,128)(2,1)S(1)}, bf16[1,192,288]{2,1,0:T(8,128)(2,1)}, u32[]{:S(2)}) %copy-start.2) | copy-done | bytes 110616
  4.1 0.0 copy-start.3
  4.1 0.7 %copy-done.3 = bf16[1,288]{1,0:T(2,128)(2,1)S(1)} copy-done((bf16[1,288]{1,0:T(2,128)(2,1)S(1)}, bf16[1,288]{1,0:T(2,128)(2,1)}, u32[]{:S(2)}) %copy-start.3) | copy-done | bytes 600
  4.8 0.0 copy-start.4
  4.8 0.7 %copy-done.4 = f32[256]{0:T(256)S(1)} copy-done((f32[256]{0:T(256)S(1)}, f32[256]{0:T(256)}, u32[]{:S(2)}) %copy-start.4) | copy-done | bytes 1048
  5.4 58.9 %shard_map.68 = (bf16[1152,256]{1,0:T(8,128)(2,1)S(1)}, bf16[256,2304]{1,0:T(8,128)(2,1)S(1)}) custom-call(bf16[192,288]{1,0:T(8,128)(2,1)S(1)} %bitcast.10, bf16[2304,256]{1,0:T(8,128)(2,1)S(1)} %bitcast.6, f32[1,256]{1,0:T(1,128)S(1)} %bitcast.11, bf16[256,2304]{1,0:T(8,128)(2,1)S(1)} %bitcast.7, bf16[1,288]{1,0:T(2,128)(2,1)S(1)} %copy-done.3), custom_call_target="tpu_custom_call" | custom-call | tf_op jit(solution)/shard_map/pallas_call | solution.py:402
  64.3 0.8 %copy.9 = bf16[1,1152,256]{2,1,0:T(8,128)(2,1)} copy(bf16[1,1152,256]{2,1,0:T(8,128)(2,1)S(1)} %bitcast.9) | data formatting | bytes 1179648
  65.1 1.0 %copy.10 = bf16[1,256,2304]{2,1,0:T(8,128)(2,1)} copy(bf16[1,256,2304]{2,1,0:T(8,128)(2,1)S(1)} %bitcast.8) | data formatting | bytes 2359296
Async XLA Ops:
  0.6 1.3 %copy-start = (bf16[1,2304,256]{2,1,0:T(8,128)(2,1)S(1)}, bf16[1,2304,256]{2,1,0:T(8,128)(2,1)}, u32[]{:S(2)}) copy-start(bf16[1,2304,256]{2,1,0:T(8,128)(2,1)} %param.6) | copy-start | bytes 3538948
  1.9 1.3 %copy-start.1 = (bf16[1,256,2304]{2,1,0:T(8,128)(2,1)S(1)}, bf16[1,256,2304]{2,1,0:T(8,128)(2,1)}, u32[]{:S(2)}) copy-start(bf16[1,256,2304]{2,1,0:T(8,128)(2,1)} %param.8) | copy-start | bytes 3538948
  3.2 0.9 %copy-start.2 = (bf16[1,192,288]{2,1,0:T(8,128)(2,1)S(1)}, bf16[1,192,288]{2,1,0:T(8,128)(2,1)}, u32[]{:S(2)}) copy-start(bf16[1,192,288]{2,1,0:T(8,128)(2,1)} %param.5) | copy-start | bytes 331780
  4.1 0.7 %copy-start.3 = (bf16[1,288]{1,0:T(2,128)(2,1)S(1)}, bf16[1,288]{1,0:T(2,128)(2,1)}, u32[]{:S(2)}) copy-start(bf16[1,288]{1,0:T(2,128)(2,1)} %bd_ref.1) | copy-start | bytes 1732
  4.8 0.7 %copy-start.4 = (f32[256]{0:T(256)S(1)}, f32[256]{0:T(256)}, u32[]{:S(2)}) copy-start(f32[256]{0:T(256)} %param.7) | copy-start | bytes 3076

commit v2 on v1

--- a/solution.py
+++ b/solution.py
@@ -9,6 +9,7 @@
 
 BETA = 4.0
 LANES = 128
+CHUNKS = 3
 MESH = pl.DeviceIdType.MESH
 F32 = jnp.float32
 BF16 = jnp.bfloat16
@@ -50,11 +51,11 @@
 
 def kernel(
     n_lat, tokens,
-    x_ref, we_hbm, be_ref, wd_hbm, bd_ref,
+    x_hbm, we_hbm, be_hbm, wd_hbm, bd_hbm,
     oe_ref, od_ref,
-    we, wdv, wd, xb, xo, xt, gb, go, pre, slope, act, act_t, act_o, ys, yr, hs, hr, gp, gp_o,
-    xs, xr, zs, zr,
-    load_sem, x_ss, x_rs, xo_rs, g_ss, g_rs, go_rs, one_ss, one_rs, xs_ss, xr_rs, zs_ss, zr_rs,
+    x_ref, be_ref, bd_ref, we, wdv, wd, xb, xo, xt, gb, go, pre, slope, act, act_t, act_o, ys, yr, hs, hr, gp, gp_o,
+    xs, xr, zs, cr, mine,
+    load_sem, x_ss, x_rs, xo_rs, g_ss, g_rs, go_rs, one_ss, one_rs, xs_ss, xr_rs, zs_ss, cr_rs,
 ):
     rows, feats = x_ref.shape
     hid = we.shape[1]
@@ -73,19 +74,32 @@
     across = 2 * z + 1 - xx
     lay_o, tok_o = 1 - lay, 1 - tok
 
-    we_load = pltpu.make_async_copy(we_hbm, we, load_sem.at[0])
-    wd_load = pltpu.make_async_copy(wd_hbm, wdv, load_sem.at[1])
-    we_load.start()
-    wd_load.start()
+    loads = [
+        pltpu.make_async_copy(src, dst, load_sem.at[i])
+        for i, (src, dst) in enumerate(
+            [(x_hbm, x_ref), (we_hbm, we), (wd_hbm, wdv), (be_hbm, be_ref), (bd_hbm, bd_ref)]
+        )
+    ]
+    for load in loads:
+        load.start()
+    x_load, we_load, wd_load, be_load, bd_load = loads
 
     barrier = pltpu.get_barrier_semaphore()
-    for d in range(1, nz):
-        pl.semaphore_signal(
-            barrier, inc=1, device_id={"latent": 2 * ((z + d) % nz) + xx}, device_id_type=MESH
-        )
-    pl.semaphore_signal(barrier, inc=1, device_id={"latent": across}, device_id_type=MESH)
-    pl.semaphore_signal(barrier, inc=1, device_id={"layer": lay_o}, device_id_type=MESH)
-    pl.semaphore_signal(barrier, inc=1, device_id={"tok": tok_o}, device_id_type=MESH)
+
+    def greet(where):
+        pl.semaphore_signal(barrier, inc=1, device_id=where, device_id_type=MESH)
+
+    greet({"latent": across})
+    greet({"layer": lay_o})
+    greet({"tok": tok_o})
+
+    @pl.when(z < nz - 1)
+    def _():
+        greet({"latent": lat + 2})
+
+    @pl.when(z > 0)
+    def _():
+        greet({"latent": lat - 2})
 
     def remote(src, dst, ss, rs, where):
         return pltpu.make_async_remote_copy(
@@ -113,120 +127,103 @@
             [block[i * rows:(i + 1) * rows] for i in range(tiles)] + [parts], axis=1
         )
 
+    size = xb.shape[1]
+    chunk = size // CHUNKS
+
+    def part(ref, *at, c):
+        return ref.at[(*at, pl.ds(c * chunk, chunk))]
+
+    def if_up(fn):
+        pl.when(z < nz - 1)(fn)
+
+    def if_down(fn):
+        pl.when(z > 0)(fn)
+
     def gather(buf, ss, rs, use, to_tok):
-        def up(j):
-            return remote(buf.at[j], buf.at[j], ss.at[0, j], rs.at[j], {"latent": lat + 2})
-
-        def down(j):
-            return remote(buf.at[j], buf.at[j], ss.at[1, j], rs.at[j], {"latent": lat - 2})
-
-        def side(j):
-            return remote(buf.at[j], buf.at[j], ss.at[2, j], rs.at[j], {"latent": across})
-
-        @pl.when(z < nz - 1)
-        def _():
-            up(lat).start()
-
-        @pl.when(z > 0)
-        def _():
-            down(lat).start()
-
-        side(lat).start()
+        def send(way, j, c):
+            where = {"latent": (lat + 2, lat - 2, across)[way]}
+            return remote(
+                part(buf, j, c=c), part(buf, j, c=c), ss.at[way, j, c], rs.at[j, c], where
+            )
+
+        for c in range(CHUNKS):
+            if_up(lambda: send(0, lat, c).start())
+            if_down(lambda: send(1, lat, c).start())
+            send(2, lat, c).start()
         to_tok(lat)
         use(lat)
 
+        def side_block(j):
+            for c in range(CHUNKS):
+                send(2, j, c).wait_recv()
+            to_tok(j)
+            use(j)
+
         def far(s):
+            pl.when(z - s >= 0)(lambda: side_block(across - 2 * s))
+            pl.when(z + s < nz)(lambda: side_block(across + 2 * s))
+
+        for s in range(1, nz):
+            for c in range(CHUNKS):
+                @pl.when(z - s >= 0)
+                def _():
+                    j = lat - 2 * s
+                    send(2, j, c).wait_recv()
+                    if_up(lambda: send(0, j, c).start())
+                    send(2, j, c).start()
+
+                @pl.when(z + s < nz)
+                def _():
+                    j = lat + 2 * s
+                    send(2, j, c).wait_recv()
+                    if_down(lambda: send(1, j, c).start())
+                    send(2, j, c).start()
+
             @pl.when(z - s >= 0)
             def _():
-                j = across - 2 * s
-                side(j).wait_recv()
-                to_tok(j)
-                use(j)
+                to_tok(lat - 2 * s)
+                use(lat - 2 * s)
 
             @pl.when(z + s < nz)
             def _():
-                j = across + 2 * s
-                side(j).wait_recv()
-                to_tok(j)
-                use(j)
-
-        for s in range(1, nz):
-            @pl.when(z - s >= 0)
-            def _():
-                j = lat - 2 * s
-                side(j).wait_recv()
-
-                @pl.when(z < nz - 1)
-                def _():
-                    up(j).start()
-
-                side(j).start()
-                to_tok(j)
-                use(j)
-
-            @pl.when(z + s < nz)
-            def _():
-                j = lat + 2 * s
-                side(j).wait_recv()
-
-                @pl.when(z > 0)
-                def _():
-                    down(j).start()
-
-                side(j).start()
-                to_tok(j)
-                use(j)
+                to_tok(lat + 2 * s)
+                use(lat + 2 * s)
 
             if s == 1:
-                side(across).wait_recv()
-                to_tok(across)
-                use(across)
+                side_block(across)
             else:
                 far(s - 1)
         far(nz - 1)
 
         def finish():
-            side(lat).wait_send()
-
-            @pl.when(z < nz - 1)
-            def _():
-                up(lat).wait_send()
-
-            @pl.when(z > 0)
-            def _():
-                down(lat).wait_send()
-
-            for s in range(1, nz):
-                @pl.when(z - s >= 0)
-                def _():
-                    j = lat - 2 * s
-                    side(j).wait_send()
-
-                    @pl.when(z < nz - 1)
+            for c in range(CHUNKS):
+                send(2, lat, c).wait_send()
+                if_up(lambda: send(0, lat, c).wait_send())
+                if_down(lambda: send(1, lat, c).wait_send())
+                for s in range(1, nz):
+                    @pl.when(z - s >= 0)
                     def _():
-                        up(j).wait_send()
-
-                @pl.when(z + s < nz)
-                def _():
-                    j = lat + 2 * s
-                    side(j).wait_send()
-
-                    @pl.when(z > 0)
+                        send(2, lat - 2 * s, c).wait_send()
+                        if_up(lambda: send(0, lat - 2 * s, c).wait_send())
+
+                    @pl.when(z + s < nz)
                     def _():
-                        down(j).wait_send()
+                        send(2, lat + 2 * s, c).wait_send()
+                        if_down(lambda: send(1, lat + 2 * s, c).wait_send())
 
         return finish
 
+    x_load.wait()
     tail = x_ref[:, main:]
     wide = jnp.concatenate([x_ref[:, :main]] + [tail] * groups, axis=1)
     xb[lat] = pack(wide.astype(F32)).astype(BF16)
     pre[...] = jnp.zeros_like(pre)
 
-    pl.semaphore_wait(barrier, nz + 2)
+    pl.semaphore_wait(barrier, 3 + (z + nz - 1) // nz + (2 * nz - 2 - z) // nz)
 
     def x_tok(i):
         return remote(
-            xb.at[half * tok_o + i], xo.at[i], x_ss.at[3, i], xo_rs.at[i], {"tok": tok_o}
+            xb.at[half * tok_o + i], xo.at[i], x_ss.at[3, i, 0], xo_rs.at[i], {"tok": tok_o}
         )
 
     def x_to_tok(j):
@@ -261,44 +258,62 @@
     ys[...] = pre[...].astype(BF16)
     y_copy = remote(ys, yr, one_ss.at[0], one_rs.at[0], {"layer": lay_o})
     y_copy.start()
+    be_load.wait()
+    bd_load.wait()
     y_copy.wait_recv()
     v = BETA * (pre[...] + yr[...].astype(F32) + be_ref[...])
     e = jnp.exp(-jnp.abs(v))
     act[...] = ((jnp.maximum(v, 0.0) + jnp.log1p(e)) / BETA).astype(BF16)
     slope[...] = jnp.where(v >= 0, 1.0, e) / (1.0 + e)
 
-    def other(k):
-        hi = z // (nz // 2)
-        m = z + hi * (nz - 1 - 2 * z)
-        if k == nz - 1:
-            return z
-        vv = nz - 1 - k - (m + k) // (nz - 1)
-        return vv + hi * (nz - 1 - 2 * vv)
-
-    def x_send(zt):
-        return remote(xs.at[zt], xr.at[zt], xs_ss.at[zt], xr_rs.at[zt], {"latent": across})
-
-    def z_send(zt):
-        return remote(zs.at[zt], zr.at[z], zs_ss.at[zt], zr_rs.at[z], {"latent": 2 * zt + xx})
-
-    def z_recv(zt):
-        return remote(zs.at[zt], zr.at[zt], zs_ss.at[zt], zr_rs.at[zt], {"latent": 2 * zt + xx})
+    order = [sign * d for d in range(nz - 1, 0, -1) for sign in (1, -1)]
+
+    def each(fn):
+        for d in order:
+            pl.when(jnp.logical_and(z + d >= 0, z + d < nz))(functools.partial(fn, d))
+
+    def x_send(zt, c):
+        return remote(
+            part(xs, zt, c=c), part(xr, zt, c=c), xs_ss.at[zt, c], xr_rs.at[zt, c],
+            {"latent": across},
+        )
+
+    def z_send(way, zt, c):
+        where = {"latent": (lat + 2, lat - 2)[way]}
+        return remote(
+            part(zs, zt, c=c), part(cr, way, zt, c=c), zs_ss.at[zt, c], cr_rs.at[way, zt, c], where
+        )
 
     def decode(j):
         return pack(jnp.dot(act[...], wd[j], preferred_element_type=F32))
 
-    for k in range(nz):
-        zt = other(k)
+    def x_out(d):
+        zt = z + d
         xs[zt] = decode(2 * zt + 1 - xx).astype(BF16)
-        x_send(zt).start()
+        for c in range(CHUNKS):
+            x_send(zt, c).start()
+
+    def z_out(d):
+        zt, way = z + d, (0 if d > 0 else 1)
+        mine[...] = decode(2 * zt + xx)
+        for c in range(CHUNKS):
+            lo = pl.ds(c * chunk, chunk)
+            x_send(zt, c).wait_recv()
+            mine[lo] += xr[zt, lo].astype(F32)
+
+            @pl.when(z > 0 if d > 0 else z < nz - 1)
+            def _():
+                z_send(way, zt, c).wait_recv()
+                mine[lo] += cr[way, zt, lo].astype(F32)
+
+            zs[zt, lo] = mine[lo].astype(BF16)
+            z_send(way, zt, c).start()
+
+    each(x_out)
+    x_out(0)
     a_copy = remote(act, act_o, one_ss.at[1], one_rs.at[1], {"tok": tok_o})
     a_copy.start()
-    for k in range(nz - 1):
-        zt = other(k)
-        mine = decode(2 * zt + xx)
-        x_send(zt).wait_recv()
-        zs[zt] = (mine + xr[zt].astype(F32)).astype(BF16)
-        z_send(zt).start()
+    each(z_out)
     total = decode(lat)
     bias = bd_ref[...].astype(F32)
     bias = jnp.concatenate([bias[:, :main]] + [bias[:, main:]] * groups, axis=1)
@@ -313,17 +328,24 @@
         xt[i] = both.T
     a_copy.wait_recv()
     act_t[...] = jnp.concatenate([act[...], act_o[...]], axis=0).T
-    x_send(z).wait_recv()
-    total += xr[z].astype(F32)
-    for k in reversed(range(nz - 1)):
-        zt = other(k)
-        z_recv(zt).wait_recv()
-        total += zr[zt].astype(F32)
+    mine[...] = total
+    for c in range(CHUNKS):
+        x_send(z, c).wait_recv()
+    mine[...] += xr[z].astype(F32)
+
+    def last(way):
+        for c in range(CHUNKS):
+            z_send(way, z, c).wait_recv()
+        mine[...] += cr[way, z].astype(F32)
+
+    if_down(lambda: last(0))
+    if_up(lambda: last(1))
+    total = mine[...]
     gb[lat] = (2.0 / tokens * total).astype(BF16)
     pre[...] = jnp.zeros_like(pre)
 
     def g_tok(j):
-        return remote(gb.at[j], go.at[j], g_ss.at[3, j], go_rs.at[j], {"tok": tok_o})
+        return remote(gb.at[j], go.at[j], g_ss.at[3, j, 0], go_rs.at[j], {"tok": tok_o})
 
     def g_to_tok(j):
         g_tok(j).start()
@@ -378,10 +400,10 @@
     a_copy.wait_send()
     h_copy.wait_send()
     p_copy.wait_send()
-    for k in range(nz):
-        x_send(other(k)).wait_send()
-    for k in range(nz - 1):
-        z_send(other(k)).wait_send()
+    for c in range(CHUNKS):
+        each(lambda d: x_send(z + d, c).wait_send())
+        x_send(z, c).wait_send()
+        each(lambda d: z_send(0 if d > 0 else 1, z + d, c).wait_send())
 
 
 def fused_shards(n_lat, resid, w_enc, b_enc, w_dec, b_dec):
@@ -398,16 +420,17 @@
     blocks_z = vm((nz, block, LANES), BF16)
     square = vm((rows, hid), BF16)
     in_vmem = pl.BlockSpec(memory_space=pltpu.VMEM)
-    anywhere = pl.BlockSpec(memory_space=pl.ANY)
+    in_hbm = pl.BlockSpec(memory_space=pltpu.HBM)
     ge, gd = pl.pallas_call(
         functools.partial(kernel, n_lat, rows * 2),
         out_shape=(
             jax.ShapeDtypeStruct((half * feats, hid), BF16),
             jax.ShapeDtypeStruct((hid, total), BF16),
         ),
-        in_specs=[in_vmem, anywhere, in_vmem, anywhere, in_vmem],
+        in_specs=[in_hbm] * 5,
         out_specs=(in_vmem, in_vmem),
         scratch_shapes=[
+            vm((rows, feats), BF16), vm((1, hid), F32), vm((1, feats), BF16),
             vm((total, hid), BF16),
             vm((hid, total), BF16),
             vm((n_lat, hid, wide), BF16),
@@ -418,15 +441,16 @@
             vm((rows, hid), F32), vm((rows, hid), F32),
             square, vm((hid, 2 * rows), BF16), square,
             square, square, square, square, square, square,
-            blocks_z, blocks_z, blocks_z, blocks_z,
-            dma((2,)),
-            dma((4, n_lat)), dma((n_lat,)), dma((half,)),
-            dma((4, n_lat)), dma((n_lat,)), dma((n_lat,)),
+            blocks_z, blocks_z, blocks_z, vm((2, nz, block, LANES), BF16),
+            vm((block, LANES), F32),
+            dma((5,)),
+            dma((4, n_lat, CHUNKS)), dma((n_lat, CHUNKS)), dma((half,)),
+            dma((4, n_lat, CHUNKS)), dma((n_lat, CHUNKS)), dma((n_lat,)),
             dma((4,)), dma((4,)),
-            dma((nz,)), dma((nz,)), dma((nz,)), dma((nz,)),
+            dma((nz, CHUNKS)), dma((nz, CHUNKS)), dma((nz, CHUNKS)), dma((2, nz, CHUNKS)),
         ],
         compiler_params=pltpu.CompilerParams(
-            collective_id=0, has_side_effects=True, vmem_limit_bytes=48 * 2**20
+            collective_id=0, has_side_effects=True, vmem_limit_bytes=67043328
         ),
     )(x, we, b_enc.reshape(1, -1), wd, b_dec)
     return ge[None], gd[None]
@@ -438,7 +462,8 @@
         return False
     if rest == 0 or rest % 32 or LANES % rest:
         return False
-    return rows % (16 * (LANES // rest)) == 0 and feats > LANES
+    fits = rows % (16 * (LANES // rest)) == 0 and feats > LANES
+    return fits and rows * feats // LANES % (16 * CHUNKS) == 0
 
 
 def solution(mesh):

time: 66.4 us -> 63.7 us (0.959)
  local copies, waits for them, and re-layouts: 6.63 us -> 3.03 us
  Pallas kernels: 58.9 us -> 59.8 us
    unnamed x12 -> x4, local copies, waits for them, and re-layouts: 6.63 us -> 3.03 us
    pallas_call x1, Pallas kernels: 58.9 us -> 59.8 us  [fused_shards(): pl.pallas_call(functools.partial(kernel, n_lat, rows * 2), out_shape=(jax...]
where the time goes in v2:
time: 63.7 us; the launch traced here: 63.5 us
  Pallas kernels  59.8 us (94%)
  local copies, waits for them, and re-layouts  3.03 us (5%)
  between operations  0.65 us (1%)
    pallas_call x1, Pallas kernels, fused_shards(): pl.pallas_call(functools.partial(kernel, n_lat, rows * 2), out_shape=(jax...  59.8 us
    unnamed x4, local copies, waits for them, and re-layouts  3.03 us

profile of v2, /device:TPU:1, one launch (start us, length us, event | category | flops | bytes accessed | tf_op | source)
XLA Modules:
  0.0 63.5 jit_solution(6427073802965155339)
XLA Ops:
  0.6 59.8 %shard_map.68 = (bf16[1152,256]{1,0:T(8,128)(2,1)}, bf16[256,2304]{1,0:T(8,128)(2,1)}) custom-call(bf16[192,288]{1,0:T(8,128)(2,1)} %bitcast.10, bf16[2304,256]{1,0:T(8,128)(2,1)} %bitcast.6, f32[1,256]{1,0:T(1,128)} %bitcast.11, bf16[256,2304]{1,0:T(8,128)(2,1)} %bitcast.7, bf16[1,288]{1,0:T(2,128)(2,1)} %bd_hbm.1), custom_call_target="tpu_custom_call" | custom-call | tf_op jit(solution)/shard_map/pallas_call | solution.py:424
  60.5 0.0 copy-start
  60.5 2.0 %copy.9 = bf16[1,1152,256]{2,1,0:T(8,128)(2,1)} copy(bf16[1,1152,256]{2,1,0:T(8,128)(2,1)} %bitcast.9) | data formatting | bytes 1179648
  62.5 0.0 copy-done
  62.5 1.0 %copy.10 = bf16[1,256,2304]{2,1,0:T(8,128)(2,1)} copy(bf16[1,256,2304]{2,1,0:T(8,128)(2,1)S(1)} %bitcast.8) | data formatting | bytes 2359296
Async XLA Ops:
  60.5 2.0 %copy-start = (bf16[256,2304]{1,0:T(8,128)(2,1)S(1)}, bf16[256,2304]{1,0:T(8,128)(2,1)}, u32[]{:S(2)}) copy-start(bf16[256,2304]{1,0:T(8,128)(2,1)} %get-tuple-element.5) | copy-start | bytes 3538948
